TPU v7x, 256 devices: a whole 4x4x8 slice. The times are simulated.
256 devices in a mesh: row: 16 (over z, core), col: 16 (over y, x).
Axes of the slice: x: 4, y: 4, z: 8, core: 2. Of those that a mesh axis runs over, the one named last changes fastest.
Arguments:
- inverse: float32 [5, 16, 5, 16, 256, 256], P(None, 'row', None, 'col')
- struct_first: int32 [32], replicated, may hold values from 0 to 79, as said below
- struct_second: int32 [16], replicated, may hold values from 0 to 79, as said below
- factor_first: float32 [32, 256, 256], P('row'), may hold values from -0.25 to 0.25
- factor_second: float32 [16, 256, 256], P('row'), may hold values from -0.25 to 0.25
- link_factor: float32 [256, 256], replicated, may hold values from -0.375 to 0.375
- dinv_first: float32 [256, 256], replicated, may hold values from -6 to 6
- dinv_second: float32 [256, 256], replicated, may hold values from -6 to 6
Outputs:
- column_first: float32 [5, 16, 256, 256], P(None, 'row', None, 'col')
- diag_first: float32 [256, 256], P(None, 'col')
- column_second: float32 [5, 16, 256, 256], P(None, 'row', None, 'col')
- link_second: float32 [256, 256], P(None, 'col')
- diag_second: float32 [256, 256], P(None, 'col')
Inputs may be any that keep to these rules, and one draw needn't show every extreme that they name: `struct_first`: distinct tile ids. `struct_second`: distinct tile ids, each of them also in struct_first.
All inputs are finite; a program needn't handle non-finite values.
Results may differ from a plain program's by a relative error of at most 0.0001.
Values sent between devices are 32-bit elements; how exact they have to be, the bound alone decides.
A program may use at most 128 MiB of HBM per device.

v0:
```python
import jax
import jax.numpy as jnp
from jax import lax
from jax.sharding import PartitionSpec as P

PRECISE = lax.Precision.HIGHEST


def body(
    inverse,
    struct_first,
    struct_second,
    factor_first,
    factor_second,
    link_factor,
    dinv_first,
    dinv_second,
):
    grid_rows = lax.axis_size("row")
    grid_cols = lax.axis_size("col")
    my_row = lax.axis_index("row")
    my_col = lax.axis_index("col")
    tile_rows, _, tile_cols, _, extent, _ = inverse.shape
    local_inv = inverse.reshape(tile_rows, tile_cols, extent, extent)
    col_width = extent // grid_cols
    offset = my_col * col_width
    col_tiles = jnp.arange(tile_cols, dtype=jnp.int32) * grid_cols + my_col
    row_tiles = jnp.arange(tile_rows, dtype=jnp.int32) * grid_rows + my_row

    def route(factor, tile_ids):
        block_in = lax.all_gather(factor, "row", axis=0, tiled=True)
        pick_col = (tile_ids[None, :] == col_tiles[:, None]).astype(jnp.float32)
        pick_row = (tile_ids[None, :] == row_tiles[:, None]).astype(jnp.float32)
        col_sel = jnp.einsum("bj,jxy->bxy", pick_col, block_in, precision=PRECISE)
        row_sel = jnp.einsum("aj,jxy->axy", pick_row, block_in, precision=PRECISE)
        return (col_sel, row_sel)

    def reduce_cols(stacked):
        summed = lax.psum(stacked, "col")
        return lax.dynamic_slice_in_dim(summed, offset, col_width, 2)

    col_first, row_first = route(factor_first, struct_first)
    product_first = jnp.einsum("abxy,byz->axz", local_inv, col_first, precision=PRECISE)
    panel_first = reduce_cols(product_first)
    owned_first = jnp.any(row_tiles[:, None] == struct_first[None, :], axis=1).astype(jnp.float32)
    column_first = -owned_first[:, None, None] * panel_first
    diag_terms = jnp.einsum("axy,axz->yz", row_first, panel_first, precision=PRECISE)
    diag_first = lax.dynamic_slice_in_dim(dinv_first, offset, col_width, 1) + lax.psum(
        diag_terms, "row"
    )
    col_second, row_second = route(factor_second, struct_second)
    link_rows = lax.dynamic_slice_in_dim(link_factor, offset, col_width, 0)
    product_second = jnp.einsum("abxy,byz->axz", local_inv, col_second, precision=PRECISE)
    product_second = product_second + jnp.einsum(
        "axw,wz->axz", column_first, link_rows, precision=PRECISE
    )
    link_term = jnp.dot(
        diag_first, link_rows, precision=PRECISE, preferred_element_type=jnp.float32
    )
    reduced = reduce_cols(jnp.concatenate([product_second, link_term[None]], axis=0))
    panel_second = reduced[:tile_rows]
    join_share = reduced[tile_rows]
    owned_second = jnp.any(row_tiles[:, None] == struct_second[None, :], axis=1).astype(jnp.float32)
    column_second = -owned_second[:, None, None] * panel_second
    turned_part = jnp.einsum("axw,axz->wz", column_first, row_second, precision=PRECISE)
    second_terms = jnp.einsum("axy,axz->yz", row_second, panel_second, precision=PRECISE)
    turned_sum, second_sum = lax.psum((turned_part, second_terms), "row")
    turned = lax.all_to_all(turned_sum, "col", split_axis=1, concat_axis=0, tiled=True)
    joined = turned + join_share
    link_second = -joined
    diag_second = lax.dynamic_slice_in_dim(dinv_second, offset, col_width, 1) + second_sum
    diag_second = diag_second + jnp.dot(
        link_factor.T, joined, precision=PRECISE, preferred_element_type=jnp.float32
    )
    out_shape = (tile_rows, 1, extent, col_width)
    return (
        column_first.reshape(out_shape),
        diag_first,
        column_second.reshape(out_shape),
        link_second,
        diag_second,
    )


def solution(mesh):
    placed = (
        P(None, "row", None, "col", None, None),
        P(),
        P(),
        P("row", None, None),
        P("row", None, None),
        P(),
        P(),
        P(),
    )
    return jax.shard_map(
        body,
        mesh=mesh,
        in_specs=placed,
        out_specs=(
            P(None, "row", None, "col"),
            P(None, "col"),
            P(None, "row", None, "col"),
            P(None, "col"),
            P(None, "col"),
        ),
        check_vma=False,
    )
```

profile of v0, /device:TPU:2, one launch (start us, length us, event | category | flops | bytes accessed | tf_op | source)
XLA Modules:
  0.0 435.4 jit_solution(15003734028828694786)
XLA Ops:
  8.0 0.7 all-gather.5.cloned.1.call-update
  8.7 1.0 constant_dynamic-slice_fusion.1
  9.8 0.8 compare_reduce_fusion.1
  10.7 58.0 %all-gather.3.cloned.1.call-done = f32[32,256,256]{2,1,0:T(8,128)} async-done(((f32[2,256,256]{2,1,0:T(8,128)}), f32[32,256,256]{2,1,0:T(8,128)}) %all-gather.3.cloned.1.call-update) | async-done | bytes 8388624 | tf_op jit(solution)/shard_map/all_gather | solution.py:31
  68.7 10.6 %fusion.2 = f32[5,256,256]{2,0,1:T(8,128)S(1)} fusion(f32[32,256,256]{2,1,0:T(8,128)} %all-gather.3.cloned.1.call-done, s32[32]{0:T(128)} %param.9, s32[5]{0:T(128)S(1)} %fusion.62), kind=kOutput, calls=%fused_computation.2 | convolution fusion | flops 125829280 | bytes 9699476 | tf_op jit(solution)/shard_map/bj,jxy->bxy/dot_general | solution.py:34
  79.3 1.5 copy.35
  80.8 9.9 %fusion.12 = f32[5,256,256]{1,2,0:T(8,128)} fusion(f32[5,1,5,1,256,256]{5,4,3,2,1,0:T(8,128)} %param.8, f32[5,256,256]{1,2,0:T(8,128)} %copy.35), kind=kOutput, calls=%fused_computation.13 | convolution fusion | flops 5033164800 | bytes 9175040 | tf_op jit(solution)/shard_map/abxy,byz->axz/dot_general | solution.py:43
  90.8 10.8 %all-reduce.6.cloned.1.call-start = ((), (), s32[]{:S(2)}) async-start(), calls=%async_computation.4 | async-start | bytes 3145728 | tf_op jit(solution)/shard_map/psum | solution.py:39
  101.6 9.4 %all-gather.5.cloned.1.call-done = f32[16,256,256]{2,1,0:T(8,128)} async-done(((f32[1,256,256]{2,1,0:T(8,128)}), f32[16,256,256]{2,1,0:T(8,128)}) %all-gather.5.cloned.1.call-update) | async-done | bytes 4194320 | tf_op jit(solution)/shard_map/all_gather | solution.py:31
  111.0 5.8 %fusion.10 = f32[5,256,256]{2,0,1:T(8,128)S(1)} fusion(f32[16,256,256]{2,1,0:T(8,128)} %all-gather.5.cloned.1.call-done, s32[16]{0:T(128)S(1)} %copy-done.4, s32[5]{0:T(128)S(1)} %fusion.62), kind=kOutput, calls=%fused_computation.10 | convolution fusion | flops 62914640 | bytes 5505108 | tf_op jit(solution)/shard_map/bj,jxy->bxy/dot_general | solution.py:34
  116.8 1.5 copy.40
  118.3 10.0 %fusion.15 = f32[5,256,256]{1,2,0:T(8,128)} fusion(f32[5,1,5,1,256,256]{5,4,3,2,1,0:T(8,128)} %param.8, f32[5,256,256]{1,2,0:T(8,128)} %copy.40), kind=kOutput, calls=%fused_computation.14 | convolution fusion | flops 5033164800 | bytes 9175040 | tf_op jit(solution)/shard_map/abxy,byz->axz/dot_general | solution.py:53
  128.3 10.7 %fusion = f32[5,256,256]{2,0,1:T(8,128)S(1)} fusion(f32[32,256,256]{2,1,0:T(8,128)} %all-gather.3.cloned.1.call-done, s32[32]{0:T(128)S(1)} %copy-done.3, s32[5]{0:T(128)S(1)} %fusion.63), kind=kOutput, calls=%fused_computation | convolution fusion | flops 125829280 | bytes 9699476 | tf_op jit(solution)/shard_map/aj,jxy->axy/dot_general | solution.py:35
  139.0 71.3 %all-reduce.4.cloned.1.call-done = f32[5,256,256]{1,2,0:T(8,128)} async-done(((f32[5,256,256]{1,2,0:T(8,128)}), f32[5,256,256]{1,2,0:T(8,128)}) %all-reduce.4.cloned.1.call-update) | async-done | bytes 1310736 | tf_op jit(solution)/shard_map/psum | solution.py:39
  210.4 1.9 fusion.22
  212.3 46.3 %psum.36 = f32[256,16]{0,1:T(8,128)S(1)} all-reduce(f32[256,16]{0,1:T(8,128)S(1)} %fusion.22), channel_id=1, replica_groups=mesh['row'=16,'col'=16] {'row'}, use_global_device_ids=true, to_apply=%region_2.0 | all-reduce | flops 4096 | bytes 32768 | tf_op jit(solution)/shard_map/psum | solution.py:48
  259.0 2.6 convolution_add_fusion
  261.6 1.2 pad_maximum_fusion
  262.9 0.9 copy-done.2
  264.2 5.8 %fusion.8 = f32[5,256,256]{2,0,1:T(8,128)S(1)} fusion(f32[16,256,256]{2,1,0:T(8,128)} %all-gather.5.cloned.1.call-done, s32[16]{0:T(128)S(1)} %copy-done.4, s32[5]{0:T(128)S(1)} %fusion.63), kind=kOutput, calls=%fused_computation.8 | convolution fusion | flops 62914640 | bytes 5505108 | tf_op jit(solution)/shard_map/aj,jxy->axy/dot_general | solution.py:35
  270.0 1.6 fusion.31
  271.6 3.2 fusion.27
  274.9 86.3 %all-reduce.6.cloned.1.call-done = f32[6,256,256]{1,2,0:T(8,128)} async-done(((f32[6,256,256]{1,2,0:T(8,128)}), f32[6,256,256]{1,2,0:T(8,128)}) %all-reduce.6.cloned.1.call-update) | async-done | bytes 1572880 | tf_op jit(solution)/shard_map/psum | solution.py:39
  361.2 1.9 convolution_bitcast_fusion.1
  363.1 48.2 %all-reduce = (f32[16,16,16]{0,2,1:T(8,128)S(1)}, f32[256,16]{0,1:T(8,128)S(1)}) all-reduce(f32[16,16,16]{0,2,1:T(8,128)S(1)} %bitcast.78, f32[256,16]{0,1:T(8,128)S(1)} %convolution_bitcast_fusion.1), channel_id=1, replica_groups=mesh['row'=16,'col'=16] {'row'}, use_global_device_ids=true, to_apply=%region_5.0 | all-reduce | flops 8192 | bytes 65536 | tf_op jit(solution)/shard_map/psum | solution.py:67
  411.3 0.7 reshape.57
  412.0 5.9 %all-to-all-start = ((f32[16,1,256]{2,1,0:T(1,128)}), f32[16,1,256]{2,1,0:T(1,128)S(1)}, u32[]{:S(2)}, u32[]{:S(2)}) async-start(f32[16,1,256]{2,1,0:T(1,128)} %reshape.57), calls=%async_computation | async-start | bytes 32768 | tf_op jit(solution)/shard_map/all_to_all | solution.py:68
  417.9 1.6 multiply_bitcast_fusion
  419.5 4.6 %all-to-all-done = f32[16,1,256]{2,1,0:T(1,128)S(1)} async-done(((f32[16,1,256]{2,1,0:T(1,128)}), f32[16,1,256]{2,1,0:T(1,128)S(1)}, u32[]{:S(2)}, u32[]{:S(2)}) %all-to-all-start) | async-done | bytes 16416 | tf_op jit(solution)/shard_map/all_to_all | solution.py:68
  424.6 0.7 reduce
  425.6 1.3 fusion.39
  426.9 1.6 fusion.25
  (30 shorter events, 2.5 us)
Async XLA Ops:
  7.2 251.4 %copy-start = (f32[256,256]{1,0:T(8,128)S(1)}, f32[256,256]{1,0:T(8,128)}, u32[]{:S(2)}) copy-start(f32[256,256]{1,0:T(8,128)} %param.13) | copy-start | bytes 786436
  7.2 61.5 %all-gather.3.cloned.1.call-start = ((), (), s32[]{:S(2)}) async-start(), calls=%async_computation.1 | async-start | bytes 8912896 | tf_op jit(solution)/shard_map/all_gather | solution.py:31
  7.9 103.0 %all-gather.5.cloned.1.call-start = ((), (), s32[]{:S(2)}) async-start(), calls=%async_computation.3 | async-start | bytes 4456448 | tf_op jit(solution)/shard_map/all_gather | solution.py:31
  8.7 201.7 %all-reduce.4.cloned.1.call-start = ((), (), s32[]{:S(2)}) async-start(), calls=%async_computation.2 | async-start | bytes 2621440 | tf_op jit(solution)/shard_map/psum | solution.py:39
  80.8 30.1 %copy-start.4 = (s32[16]{0:T(128)S(1)}, s32[16]{0:T(128)}, u32[]{:S(2)}) copy-start(s32[16]{0:T(128)} %param.10) | copy-start | bytes 196
  90.8 270.4 %all-reduce.6.cloned.1.call-start = ((), (), s32[]{:S(2)}) async-start(), calls=%async_computation.4 | async-start | bytes 3145728 | tf_op jit(solution)/shard_map/psum | solution.py:39
  118.3 10.0 %copy-start.3 = (s32[32]{0:T(128)S(1)}, s32[32]{0:T(128)}, u32[]{:S(2)}) copy-start(s32[32]{0:T(128)} %param.9) | copy-start | bytes 388
  258.5 4.3 copy-start.1
  262.9 1.0 copy-start.2
  412.0 12.1 %all-to-all-start = ((f32[16,1,256]{2,1,0:T(1,128)}), f32[16,1,256]{2,1,0:T(1,128)S(1)}, u32[]{:S(2)}, u32[]{:S(2)}) async-start(f32[16,1,256]{2,1,0:T(1,128)} %reshape.57), calls=%async_computation | async-start | bytes 32768 | tf_op jit(solution)/shard_map/all_to_all | solution.py:68
Sparse Core Ops, SparseCore 0:
  9.8 58.7 all-gather.2
  70.5 40.4 all-gather.4
  114.2 96.1 all-reduce.3
  263.0 98.1 all-reduce.5
where the time goes:
time: 444 us; the launch traced here: 435 us
  waiting for transfers between devices  231 us (52%)
  blocking collectives  94.4 us (21%)
  matrix products  64.5 us (15%)
  starting transfers between devices  16.8 us (4%)
  between operations  14.3 us (3%)
  other arithmetic  7.53 us (2%)
  local copies, waits for them, and re-layouts  6.73 us (2%)
    psum x2, waiting for transfers between devices, reduce_cols(): summed = lax.psum(stacked, 'col')  158 us
    all_gather x2, waiting for transfers between devices, route(): block_in = lax.all_gather(factor, 'row', axis=0, tiled=True)  67.4 us
    psum x1, blocking collectives, body(): turned_sum, second_sum = lax.psum((turned_part, second_terms), 'row')  48.2 us
    psum x1, blocking collectives, body(): lax.psum(diag_terms, 'row')  46.3 us
    dot_general x2, matrix products, route(): row_sel = jnp.einsum('aj,jxy->axy', pick_row, block_in, precision=PRECISE)  16.6 us
    dot_general x2, matrix products, route(): col_sel = jnp.einsum('bj,jxy->bxy', pick_col, block_in, precision=PRECISE)  16.5 us
    psum x2, starting transfers between devices, reduce_cols(): summed = lax.psum(stacked, 'col')  10.8 us
    dot_general x1, matrix products, body(): jnp.einsum('abxy,byz->axz', local_inv, col_second, precision=PRECISE)  9.96 us
  transfers between devices with their start and end apart: 5, of which 5 were waited for; matrix products, arithmetic and copies ran while one was open for 15% of the time, Pallas kernels for 0%

commit v1 on v0

--- a/solution.py
+++ b/solution.py
@@ -28,7 +28,9 @@
     row_tiles = jnp.arange(tile_rows, dtype=jnp.int32) * grid_rows + my_row
 
     def route(factor, tile_ids):
-        block_in = lax.all_gather(factor, "row", axis=0, tiled=True)
+        block_in = jnp.concatenate(
+            lax.all_to_all(jnp.stack([factor] * lax.axis_size("row")), "row", 0, 0), axis=0
+        )
         pick_col = (tile_ids[None, :] == col_tiles[:, None]).astype(jnp.float32)
         pick_row = (tile_ids[None, :] == row_tiles[:, None]).astype(jnp.float32)
         col_sel = jnp.einsum("bj,jxy->bxy", pick_col, block_in, precision=PRECISE)

time: 444 us -> 578 us (1.30); the launches traced: 435 us -> 576 us
  blocking collectives: 94.4 us -> 288 us
  waiting for transfers between devices: 231 us -> 167 us
  local copies, waits for them, and re-layouts: 6.73 us -> 35.6 us
  matrix products: 64.5 us -> 53.5 us
    all_to_all x0 -> x1, blocking collectives: none -> 193 us  [route(): lax.all_to_all(jnp.stack([factor] * lax.axis_size('row')), 'row', 0, 0)]
    all_gather x2 -> x0, waiting for transfers between devices: 67.4 us -> none  [route(): block_in = lax.all_gather(factor, 'row', axis=0, tiled=True)]
    all_to_all x0 -> x1, waiting for transfers between devices: none -> 57.1 us  [route(): lax.all_to_all(jnp.stack([factor] * lax.axis_size('row')), 'row', 0, 0)]
    psum x2, waiting for transfers between devices: 158 us -> 106 us  [reduce_cols(): summed = lax.psum(stacked, 'col')]
    reshape x0 -> x1, local copies, waits for them, and re-layouts: none -> 10.9 us  [route(): jnp.concatenate(lax.all_to_all(jnp.stack([factor] * lax.axis_size('row'))...]
    psum x2, starting transfers between devices: 10.8 us -> 0.48 us  [reduce_cols(): summed = lax.psum(stacked, 'col')]
    another operation x0 -> x2, local copies, waits for them, and re-layouts: none -> 8.82 us  [route(): jnp.stack([factor] * lax.axis_size('row'))]
    all_to_all x0 -> x1, local copies, waits for them, and re-layouts: none -> 8.58 us  [route(): lax.all_to_all(jnp.stack([factor] * lax.axis_size('row')), 'row', 0, 0)]
  transfers between devices with their start and end apart: 5 -> 4, of which waited for: 5 -> 4; matrix products, arithmetic and copies ran while one was open for 15% -> 12% of each run, Pallas kernels for 0% -> 0%
where the time goes in v1:
time: 578 us; the launch traced here: 576 us
  blocking collectives  288 us (50%)
  waiting for transfers between devices  167 us (29%)
  matrix products  53.5 us (9%)
  local copies, waits for them, and re-layouts  35.6 us (6%)
  between operations  14.2 us (2%)
  starting transfers between devices  11.1 us (2%)
  other arithmetic  6.87 us (1%)
    all_to_all x1, blocking collectives, route(): lax.all_to_all(jnp.stack([factor] * lax.axis_size('row')), 'row', 0, 0)  193 us
    psum x2, waiting for transfers between devices, reduce_cols(): summed = lax.psum(stacked, 'col')  106 us
    all_to_all x1, waiting for transfers between devices, route(): lax.all_to_all(jnp.stack([factor] * lax.axis_size('row')), 'row', 0, 0)  57.1 us
    psum x1, blocking collectives, body(): turned_sum, second_sum = lax.psum((turned_part, second_terms), 'row')  48.2 us
    psum x1, blocking collectives, body(): lax.psum(diag_terms, 'row')  46.3 us
  transfers between devices with their start and end apart: 4, of which 4 were waited for; matrix products, arithmetic and copies ran while one was open for 12% of the time, Pallas kernels for 0%

profile of v1, /device:TPU:2, one launch (start us, length us, event | category | flops | bytes accessed | tf_op | source)
XLA Modules:
  0.0 576.4 jit_solution(18099234665986417335)
XLA Ops:
  7.2 1.5 copy.48
  8.7 6.4 %stack.4 = f32[16,2,256,256]{3,1,2,0:T(2,128)} broadcast(f32[2,256,256]{2,0,1:T(2,128)S(1)} %copy.48), dimensions={1,2,3} | broadcast | bytes 8912896 | tf_op jit(solution)/shard_map/stack | solution.py:32
  15.1 193.3 %all_to_all.29 = f32[16,2,256,256]{3,1,2,0:T(2,128)} all-to-all(f32[16,2,256,256]{3,1,2,0:T(2,128)} %stack.4), channel_id=1, replica_groups=mesh['row'=16,'col'=16] {'row'}, dimensions={0} | all-to-all | bytes 16777216 | tf_op jit(solution)/shard_map/all_to_all | solution.py:32
  208.4 2.4 stack.5
  210.8 4.7 all-to-all-start.1
  216.1 8.6 %copy.49 = f32[16,2,256,256]{3,1,0,2:T(2,128)} copy(f32[16,2,256,256]{3,1,2,0:T(2,128)} %all_to_all.29) | data formatting | bytes 16777216 | tf_op jit(solution)/shard_map/all_to_all | solution.py:32
  224.7 10.9 %reshape.53 = f32[32,256,256]{2,0,1:T(8,128)} reshape(f32[16,2,256,256]{3,1,0,2:T(2,128)} %copy.49) | data formatting | bytes 16777216 | tf_op jit(solution)/shard_map/reshape | solution.py:31
  235.5 5.2 fusion.42
  240.7 1.6 copy.50
  242.3 10.0 %fusion.10 = f32[5,256,256]{1,2,0:T(8,128)} fusion(f32[5,1,5,1,256,256]{5,4,3,2,1,0:T(8,128)} %param.8, f32[5,256,256]{1,2,0:T(8,128)} %copy.50), kind=kOutput, calls=%fused_computation.11 | convolution fusion | flops 5033164800 | bytes 9175040 | tf_op jit(solution)/shard_map/abxy,byz->axz/dot_general | solution.py:45
  252.5 57.1 %all-to-all-done.1 = f32[16,1,256,256]{3,2,1,0:T(8,128)} async-done(((f32[16,1,256,256]{3,2,1,0:T(8,128)}), f32[16,1,256,256]{3,2,1,0:T(8,128)}, u32[]{:S(2)}, u32[]{:S(2)}) %all-to-all-start.1) | async-done | bytes 4194336 | tf_op jit(solution)/shard_map/all_to_all | solution.py:32
  309.7 5.9 %fusion.6 = f32[5,256,256]{2,0,1:T(8,128)S(1)} fusion(f32[16,1,256,256]{3,2,1,0:T(8,128)} %all-to-all-done.1, s32[16]{0:T(128)S(1)} %copy-done.6, s32[5]{0:T(128)S(1)} %fusion.62), kind=kOutput, calls=%fused_computation.6 | convolution fusion | flops 62914640 | bytes 5505108 | tf_op jit(solution)/shard_map/bj,jxy->bxy/dot_general | solution.py:36
  315.5 1.5 copy.54
  317.1 9.9 %fusion.13 = f32[5,256,256]{1,2,0:T(8,128)} fusion(f32[5,1,5,1,256,256]{5,4,3,2,1,0:T(8,128)} %param.8, f32[5,256,256]{1,2,0:T(8,128)} %copy.54), kind=kOutput, calls=%fused_computation.12 | convolution fusion | flops 5033164800 | bytes 9175040 | tf_op jit(solution)/shard_map/abxy,byz->axz/dot_general | solution.py:55
  327.0 5.2 fusion.40
  332.2 19.3 %all-reduce.4.cloned.1.call-done = f32[5,256,256]{1,2,0:T(8,128)} async-done(((f32[5,256,256]{1,2,0:T(8,128)}), f32[5,256,256]{1,2,0:T(8,128)}) %all-reduce.4.cloned.1.call-update) | async-done | bytes 1310736 | tf_op jit(solution)/shard_map/psum | solution.py:41
  351.4 1.9 fusion.20
  353.3 46.3 %psum.36 = f32[256,16]{0,1:T(8,128)S(1)} all-reduce(f32[256,16]{0,1:T(8,128)S(1)} %fusion.20), channel_id=1, replica_groups=mesh['row'=16,'col'=16] {'row'}, use_global_device_ids=true, to_apply=%region_2.0 | all-reduce | flops 4096 | bytes 32768 | tf_op jit(solution)/shard_map/psum | solution.py:50
  400.0 2.6 convolution_add_fusion
  402.6 1.2 pad_maximum_fusion
  403.9 0.9 copy-done.4
  405.2 5.8 %fusion.4 = f32[5,256,256]{2,0,1:T(8,128)S(1)} fusion(f32[16,1,256,256]{3,2,1,0:T(8,128)} %all-to-all-done.1, s32[16]{0:T(128)S(1)} %copy-done.6, s32[5]{0:T(128)S(1)} %fusion.63), kind=kOutput, calls=%fused_computation.4 | convolution fusion | flops 62914640 | bytes 5505108 | tf_op jit(solution)/shard_map/aj,jxy->axy/dot_general | solution.py:37
  411.1 1.6 fusion.29
  412.7 3.2 fusion.25
  415.9 86.4 %all-reduce.6.cloned.1.call-done = f32[6,256,256]{1,2,0:T(8,128)} async-done(((f32[6,256,256]{1,2,0:T(8,128)}), f32[6,256,256]{1,2,0:T(8,128)}) %all-reduce.6.cloned.1.call-update) | async-done | bytes 1572880 | tf_op jit(solution)/shard_map/psum | solution.py:41
  502.3 1.9 convolution_bitcast_fusion.1
  504.2 48.2 %all-reduce = (f32[16,16,16]{0,2,1:T(8,128)S(1)}, f32[256,16]{0,1:T(8,128)S(1)}) all-reduce(f32[16,16,16]{0,2,1:T(8,128)S(1)} %bitcast.88, f32[256,16]{0,1:T(8,128)S(1)} %convolution_bitcast_fusion.1), channel_id=1, replica_groups=mesh['row'=16,'col'=16] {'row'}, use_global_device_ids=true, to_apply=%region_5.0 | all-reduce | flops 8192 | bytes 65536 | tf_op jit(solution)/shard_map/psum | solution.py:69
  553.1 5.9 %all-to-all-start.2 = ((f32[16,1,256]{2,1,0:T(1,128)}), f32[16,1,256]{2,1,0:T(1,128)S(1)}, u32[]{:S(2)}, u32[]{:S(2)}) async-start(f32[16,1,256]{2,1,0:T(1,128)} %reshape.70), calls=%async_computation.2 | async-start | bytes 32768 | tf_op jit(solution)/shard_map/all_to_all | solution.py:70
  559.0 1.6 multiply_bitcast_fusion
  560.6 4.6 all-to-all-done.2
  566.7 1.3 fusion.37
  568.0 1.6 fusion.23
  (36 shorter events, 3.9 us)
Async XLA Ops:
  7.2 392.4 %copy-start = (f32[256,256]{1,0:T(8,128)S(1)}, f32[256,256]{1,0:T(8,128)}, u32[]{:S(2)}) copy-start(f32[256,256]{1,0:T(8,128)} %param.13) | copy-start | bytes 786436
  15.1 193.3 %copy-start.1 = (f32[1,256,256]{2,1,0:T(8,128)S(1)}, f32[1,256,256]{2,1,0:T(8,128)}, u32[]{:S(2)}) copy-start(f32[1,256,256]{2,1,0:T(8,128)} %param.12) | copy-start | bytes 786436
  210.8 4.9 copy-start.3
  210.8 5.1 copy-start.5
  210.8 98.9 %all-to-all-start.1 = ((f32[16,1,256,256]{3,2,1,0:T(8,128)}), f32[16,1,256,256]{3,2,1,0:T(8,128)}, u32[]{:S(2)}, u32[]{:S(2)}) async-start(f32[16,1,256,256]{3,2,1,0:T(8,128)} %stack.5), calls=%async_computation.1 | async-start | bytes 8388608 | tf_op jit(solution)/shard_map/all_to_all | solution.py:32
  215.5 136.0 %all-reduce.4.cloned.1.call-start = ((), (), s32[]{:S(2)}) async-start(), calls=%async_computation.3 | async-start | bytes 2621440 | tf_op jit(solution)/shard_map/psum | solution.py:41
  242.3 67.4 %copy-start.6 = (s32[16]{0:T(128)S(1)}, s32[16]{0:T(128)}, u32[]{:S(2)}) copy-start(s32[16]{0:T(128)} %param.10) | copy-start | bytes 196
  252.3 250.0 %all-reduce.6.cloned.1.call-start = ((), (), s32[]{:S(2)}) async-start(), calls=%async_computation.4 | async-start | bytes 3145728 | tf_op jit(solution)/shard_map/psum | solution.py:41
  399.6 4.3 copy-start.2
  403.9 1.0 copy-start.4
  553.1 12.1 %all-to-all-start.2 = ((f32[16,1,256]{2,1,0:T(1,128)}), f32[16,1,256]{2,1,0:T(1,128)S(1)}, u32[]{:S(2)}, u32[]{:S(2)}) async-start(f32[16,1,256]{2,1,0:T(1,128)} %reshape.70), calls=%async_computation.2 | async-start | bytes 32768 | tf_op jit(solution)/shard_map/all_to_all | solution.py:70
Sparse Core Ops, SparseCore 0:
  252.4 98.9 all-reduce.3
  404.0 98.1 all-reduce.5
